TPU v7x, 1024 devices: a whole 4x4x32 slice. The times are simulated.
1024 devices in a mesh: band: 16 (over z_hi, x, core), pw: 64 (over z_lo, y).
Axes of the slice: x: 4, y: 4, z: 32 (z_hi: 2, z_lo: 16; z = z_hi * 16 + z_lo), core: 2. Of those that a mesh axis runs over, the one named last changes fastest.
Arguments:
- coeffs: bfloat16 [2, 64, 8192, 256], P(None, None, ('band', 'pw')), may hold values from -6 to 6
- rotation_matrix: bfloat16 [2, 64, 32], replicated, may hold values from -0.5 to 0.5
- stick_length: int32 [8192], replicated, may hold values from 64 to 256
- stick_column: int32 [8192], replicated, may hold values from 0 to 65535, as said below
- plane_index: int32 [128], replicated, may hold values from 0 to 255, as said below
- occupation: int32 [32], P('band'), may hold values from 0 to 2
Outputs:
- density: float32 [128, 256, 256], P('pw')
Inputs may be any that keep to these rules, and one draw needn't show every extreme that they name: `stick_column`: distinct column numbers. `plane_index`: distinct plane numbers.
All inputs are finite; a program needn't handle non-finite values.
Results may differ from a plain program's by a relative error of at most 0.003.
Values may be sent and summed in bfloat16 or wider, within the bound.
A program may use at most 64 MiB of HBM per device.

v0:
```python
import math

import jax
import jax.numpy as jnp
from jax import lax
from jax.sharding import PartitionSpec as P


def tables(grid_len, indices):
    product = jnp.arange(grid_len, dtype=jnp.int32)[:, None] * indices[None, :] % grid_len
    angles = 2.0 * math.pi / grid_len * product.astype(jnp.float32)
    return (jnp.cos(angles).astype(jnp.bfloat16), jnp.sin(angles).astype(jnp.bfloat16))


def contract(form, left, right):
    return jnp.einsum(form, left, right, preferred_element_type=jnp.float32)


def rotate(coeff_part, rotation_matrix):
    in_count = rotation_matrix.shape[1]
    out_count = rotation_matrix.shape[2]
    rotation = jnp.concatenate(
        [
            jnp.concatenate([rotation_matrix[0], rotation_matrix[1]], 1),
            jnp.concatenate([-rotation_matrix[1], rotation_matrix[0]], 1),
        ],
        0,
    )
    flattened = coeff_part.reshape(2 * in_count, -1)
    result = jnp.dot(rotation.T, flattened, preferred_element_type=jnp.float32)
    return result.reshape((2, out_count) + coeff_part.shape[2:]).astype(jnp.bfloat16)


def z_transform(rotated, lengths, plane_index):
    grid_len = rotated.shape[3]
    count = plane_index.shape[0]
    live_mask = (jnp.arange(grid_len, dtype=jnp.int32)[None, :] < lengths[:, None]).astype(
        jnp.bfloat16
    )
    masked = rotated * live_mask
    cos_table, sin_table = tables(grid_len, plane_index)
    weight = jnp.concatenate(
        [jnp.concatenate([cos_table, sin_table], 1), jnp.concatenate([-sin_table, cos_table], 1)], 0
    )
    stacked = jnp.concatenate([masked[0], masked[1]], axis=-1)
    amplitude = contract("bsj,jk->bsk", stacked, weight)
    amp_real = amplitude[..., :count]
    amp_imag = amplitude[..., count:]
    shift = (lengths // 2)[:, None] * plane_index[None, :] % grid_len
    phase = -2.0 * math.pi / grid_len * shift.astype(jnp.float32)
    phase_cos = jnp.cos(phase)
    phase_sin = jnp.sin(phase)
    out_real = amp_real * phase_cos - amp_imag * phase_sin
    out_imag = amp_real * phase_sin + amp_imag * phase_cos
    result = jnp.stack([out_real, out_imag])
    return jnp.swapaxes(result, 2, 3).astype(jnp.bfloat16)


def plane_power(values, columns, grid_len):
    shape = values.shape
    pairs = jnp.moveaxis(values.reshape(2, shape[1] * shape[2], shape[3]), 1, 0)
    cos_table, sin_table = tables(grid_len, jnp.arange(grid_len, dtype=jnp.int32))

    def one_plane(stick_values):
        flattened = (
            jnp.zeros((2, grid_len * grid_len), jnp.bfloat16).at[:, columns].set(stick_values)
        )
        planes = flattened.reshape(2, grid_len, grid_len)
        half_real = (
            contract("xy,yk->xk", planes[0], cos_table)
            - contract("xy,yk->xk", planes[1], sin_table)
        ).astype(jnp.bfloat16)
        half_imag = (
            contract("xy,yk->xk", planes[0], sin_table)
            + contract("xy,yk->xk", planes[1], cos_table)
        ).astype(jnp.bfloat16)
        wave_real = contract("xq,xk->qk", cos_table, half_real) - contract(
            "xq,xk->qk", sin_table, half_imag
        )
        wave_imag = contract("xq,xk->qk", sin_table, half_real) + contract(
            "xq,xk->qk", cos_table, half_imag
        )
        return wave_real * wave_real + wave_imag * wave_imag

    powers = lax.map(one_plane, pairs)
    return powers.reshape(shape[1], shape[2], grid_len, grid_len)


def shards(coeffs, rotation_matrix, stick_length, stick_column, plane_index, occupation):
    band_count = lax.axis_size("band")
    pw_count = lax.axis_size("pw")
    pw_index = lax.axis_index("pw")
    local_sticks = coeffs.shape[2]
    grid_len = coeffs.shape[3]
    length_table = stick_length.reshape(band_count, pw_count, local_sticks)
    columns = jnp.transpose(
        stick_column.reshape(band_count, pw_count, local_sticks), (1, 0, 2)
    ).reshape(-1)
    rotated = rotate(coeffs, rotation_matrix)
    norm_factor = 1.0 / float(occupation.shape[0] * band_count * stick_column.shape[0] * grid_len)
    grouped = lax.all_to_all(rotated, "band", split_axis=1, concat_axis=2, tiled=True)
    group_lengths = lax.dynamic_index_in_dim(length_table, pw_index, 1, False).reshape(-1)
    z_values = z_transform(grouped, group_lengths, plane_index)
    magnitudes = plane_power(
        lax.all_to_all(z_values, "pw", split_axis=2, concat_axis=3, tiled=True), columns, grid_len
    )
    local_sum = jnp.einsum("b,bzxy->zxy", occupation.astype(jnp.float32), magnitudes) * norm_factor
    return lax.psum(local_sum, "band")


def solution(mesh):
    return jax.shard_map(
        shards,
        mesh=mesh,
        in_specs=(P(None, None, ("band", "pw"), None), P(), P(), P(), P(), P("band")),
        out_specs=P("pw", None, None),
        check_vma=False,
    )
```

profile of v0, /device:TPU:1, one launch (start us, length us, event | category | flops | bytes accessed | tf_op | source)
XLA Modules:
  0.0 782.8 jit_solution(13717281067602088174)
XLA Ops:
  8.0 1.1 copy.33
  10.6 32.3 %all-to-all-start = ((bf16[2,32,8,256]{3,2,0,1:T(8,128)(2,1)}), bf16[2,32,8,256]{3,2,0,1:T(8,128)(2,1)S(1)}, u32[]{:S(2)}, u32[]{:S(2)}) async-start(bf16[2,32,8,256]{3,2,0,1:T(8,128)(2,1)} %copy.22), calls=%async_computation | async-start | bytes 524288 | tf_op jit(solution)/shard_map/all_to_all | solution.py:101
  44.2 1.2 fusion.80
  45.4 1.2 sine_convert_fusion.5
  47.6 22.2 %all-to-all-done = bf16[2,32,8,256]{3,2,0,1:T(8,128)(2,1)S(1)} async-done(((bf16[2,32,8,256]{3,2,0,1:T(8,128)(2,1)}), bf16[2,32,8,256]{3,2,0,1:T(8,128)(2,1)S(1)}, u32[]{:S(2)}, u32[]{:S(2)}) %all-to-all-start) | async-done | bytes 262176 | tf_op jit(solution)/shard_map/all_to_all | solution.py:101
  71.0 29.5 %all-to-all-start.1 = ((bf16[2,2,128,128]{3,1,0,2:T(2,128)(2,1)}), bf16[2,2,128,128]{3,1,0,2:T(2,128)(2,1)S(1)}, u32[]{:S(2)}, u32[]{:S(2)}) async-start(bf16[2,2,128,128]{3,1,0,2:T(2,128)(2,1)} %copy.24), calls=%async_computation.1 | async-start | bytes 262144 | tf_op jit(solution)/shard_map/all_to_all | solution.py:105
  102.2 20.6 %all-to-all-done.1 = bf16[2,2,128,128]{3,1,0,2:T(2,128)(2,1)S(1)} async-done(((bf16[2,2,128,128]{3,1,0,2:T(2,128)(2,1)}), bf16[2,2,128,128]{3,1,0,2:T(2,128)(2,1)S(1)}, u32[]{:S(2)}, u32[]{:S(2)}) %all-to-all-start.1) | async-done | bytes 131104 | tf_op jit(solution)/shard_map/all_to_all | solution.py:105
  122.9 248.5 %while.12 = (s32[]{:T(128)}, bf16[4,256,256]{1,2,0:T(8,128)(2,1)S(1)}, s32[8192]{0:T(1024)S(1)}, bf16[4,2,8192]{2,0,1:T(4,128)(2,1)S(1)}, s32[]{:T(128)}, /*index=5*/bf16[]{:T(256)}) while((s32[]{:T(128)}, bf16[4,256,256]{1,2,0:T(8,128)(2,1)S(1)}, s32[8192]{0:T(1024)S(1)}, bf16[4,2,8192]{2,0,1:T(4,128)(2,1)S(1)}, ...), condition=%wide.region_2.3_spmd.clone.clone, body=%wide.region_0.2_spmd.clone.clone.sunk | while | flops 276914176 | bytes 7798863 | solution.py:85
  124.3 30.1 %scatter_custom_fusion.6 = bf16[2,65536]{0,1:T(8,128)(2,1)} fusion(s32[8192]{0:T(1024)S(1)} %bitcast.108, bf16[]{:T(256)} %constant.62.clone.3..sunk, bf16[1,2,8192]{1,2,0:T(8,128)(2,1)S(1)} %copy.37), kind=kCustom, calls=%fused_computation.5.clone.1 | custom fusion | bytes 2359298 | tf_op jit(solution)/shard_map/while/body/eval_jaxpr/scatter | solution.py:66
  154.4 21.5 %slice_reduce_fusion.3 = (bf16[65536]{0:T(1024)(128)(2,1)S(1)}, bf16[65536]{0:T(1024)(128)(2,1)S(1)}) fusion(bf16[2,65536]{0,1:T(8,128)(2,1)} %scatter_custom_fusion.6), kind=kLoop, calls=%fused_computation.3.clone.1 | loop fusion | bytes 524288 | tf_op jit(solution)/shard_map/while/body/eval_jaxpr/slice | solution.py:71
  179.4 1.1 fusion.124
  181.7 1.1 fusion.128
  182.8 1.1 fusion.129
  184.0 1.1 fusion.130
  186.3 30.1 %scatter_custom_fusion.6 = bf16[2,65536]{0,1:T(8,128)(2,1)} fusion(s32[8192]{0:T(1024)S(1)} %bitcast.108, bf16[]{:T(256)} %constant.62.clone.3..sunk, bf16[1,2,8192]{1,2,0:T(8,128)(2,1)S(1)} %copy.37), kind=kCustom, calls=%fused_computation.5.clone.1 | custom fusion | bytes 2359298 | tf_op jit(solution)/shard_map/while/body/eval_jaxpr/scatter | solution.py:66
  216.5 21.5 %slice_reduce_fusion.3 = (bf16[65536]{0:T(1024)(128)(2,1)S(1)}, bf16[65536]{0:T(1024)(128)(2,1)S(1)}) fusion(bf16[2,65536]{0,1:T(8,128)(2,1)} %scatter_custom_fusion.6), kind=kLoop, calls=%fused_computation.3.clone.1 | loop fusion | bytes 524288 | tf_op jit(solution)/shard_map/while/body/eval_jaxpr/slice | solution.py:71
  241.5 1.1 fusion.124
  243.8 1.1 fusion.128
  244.9 1.1 fusion.129
  246.0 1.1 fusion.130
  248.4 30.1 %scatter_custom_fusion.6 = bf16[2,65536]{0,1:T(8,128)(2,1)} fusion(s32[8192]{0:T(1024)S(1)} %bitcast.108, bf16[]{:T(256)} %constant.62.clone.3..sunk, bf16[1,2,8192]{1,2,0:T(8,128)(2,1)S(1)} %copy.37), kind=kCustom, calls=%fused_computation.5.clone.1 | custom fusion | bytes 2359298 | tf_op jit(solution)/shard_map/while/body/eval_jaxpr/scatter | solution.py:66
  278.5 21.5 %slice_reduce_fusion.3 = (bf16[65536]{0:T(1024)(128)(2,1)S(1)}, bf16[65536]{0:T(1024)(128)(2,1)S(1)}) fusion(bf16[2,65536]{0,1:T(8,128)(2,1)} %scatter_custom_fusion.6), kind=kLoop, calls=%fused_computation.3.clone.1 | loop fusion | bytes 524288 | tf_op jit(solution)/shard_map/while/body/eval_jaxpr/slice | solution.py:71
  303.5 1.1 fusion.124
  305.8 1.1 fusion.128
  308.1 1.1 fusion.130
  310.5 30.1 %scatter_custom_fusion.6 = bf16[2,65536]{0,1:T(8,128)(2,1)} fusion(s32[8192]{0:T(1024)S(1)} %bitcast.108, bf16[]{:T(256)} %constant.62.clone.3..sunk, bf16[1,2,8192]{1,2,0:T(8,128)(2,1)S(1)} %copy.37), kind=kCustom, calls=%fused_computation.5.clone.1 | custom fusion | bytes 2359298 | tf_op jit(solution)/shard_map/while/body/eval_jaxpr/scatter | solution.py:66
  340.6 21.5 %slice_reduce_fusion.3 = (bf16[65536]{0:T(1024)(128)(2,1)S(1)}, bf16[65536]{0:T(1024)(128)(2,1)S(1)}) fusion(bf16[2,65536]{0,1:T(8,128)(2,1)} %scatter_custom_fusion.6), kind=kLoop, calls=%fused_computation.3.clone.1 | loop fusion | bytes 524288 | tf_op jit(solution)/shard_map/while/body/eval_jaxpr/slice | solution.py:71
  365.6 1.1 fusion.124
  367.9 1.1 fusion.128
  370.2 1.1 fusion.130
  373.4 400.7 %all-reduce.2.cloned.1.call-done = f32[2,256,256]{2,1,0:T(8,128)} async-done(((f32[2,256,256]{2,1,0:T(8,128)}), f32[2,256,256]{2,1,0:T(8,128)}) %all-reduce.2.cloned.1.call-update) | async-done | bytes 524304 | tf_op jit(solution)/shard_map/psum | solution.py:108
  774.0 1.9 copy.48
  (70 shorter events, 35.4 us)
Async XLA Ops:
  10.6 59.2 %all-to-all-start = ((bf16[2,32,8,256]{3,2,0,1:T(8,128)(2,1)}), bf16[2,32,8,256]{3,2,0,1:T(8,128)(2,1)S(1)}, u32[]{:S(2)}, u32[]{:S(2)}) async-start(bf16[2,32,8,256]{3,2,0,1:T(8,128)(2,1)} %copy.22), calls=%async_computation | async-start | bytes 524288 | tf_op jit(solution)/shard_map/all_to_all | solution.py:101
  71.0 51.8 %all-to-all-start.1 = ((bf16[2,2,128,128]{3,1,0,2:T(2,128)(2,1)}), bf16[2,2,128,128]{3,1,0,2:T(2,128)(2,1)S(1)}, u32[]{:S(2)}, u32[]{:S(2)}) async-start(bf16[2,2,128,128]{3,1,0,2:T(2,128)(2,1)} %copy.24), calls=%async_computation.1 | async-start | bytes 262144 | tf_op jit(solution)/shard_map/all_to_all | solution.py:105
  100.5 673.6 %all-reduce.2.cloned.1.call-start = ((), (), s32[]{:S(2)}) async-start(), calls=%async_computation.2 | async-start | bytes 1048576 | tf_op jit(solution)/shard_map/psum | solution.py:108
  122.9 248.9 %copy-start = (s32[2]{0:T(128)S(1)}, s32[2]{0:T(128)}, u32[]{:S(2)}) copy-start(s32[2]{0:T(128)} %param.13) | copy-start | bytes 28
Sparse Core Ops, SparseCore 0:
  373.5 400.5 all-reduce.1
where the time goes:
time: 783 us
  waiting for transfers between devices  444 us (57%)
  local copies, waits for them, and re-layouts  220 us (28%)
  starting transfers between devices  61.8 us (8%)
  matrix products  37.4 us (5%)
  between operations  13.6 us (2%)
    psum x1, waiting for transfers between devices, shards(): return lax.psum(local_sum, 'band')  401 us
    scatter x4, local copies, waits for them, and re-layouts, one_plane(): jnp.zeros((2, grid_len * grid_len), jnp.bfloat16).at[:, columns]  121 us
    slice x4, local copies, waits for them, and re-layouts, one_plane(): planes[1]  86 us
    dot_general x33, matrix products, contract(): return jnp.einsum(form, left, right, preferred_element_type=jnp.float32)  36.4 us
    all_to_all x1, starting transfers between devices, shards(): lax.all_to_all(rotated, 'band', split_axis=1, concat_axis=2, tiled=True)  32.3 us
    all_to_all x1, starting transfers between devices, shards(): lax.all_to_all(z_values, 'pw', split_axis=2, concat_axis=3, tiled=True)  29.5 us
    all_to_all x1, waiting for transfers between devices, shards(): lax.all_to_all(rotated, 'band', split_axis=1, concat_axis=2, tiled=True)  22.2 us
    all_to_all x1, waiting for transfers between devices, shards(): lax.all_to_all(z_values, 'pw', split_axis=2, concat_axis=3, tiled=True)  20.6 us
  transfers between devices with their start and end apart: 3, of which 3 were waited for; matrix products, arithmetic and copies ran while one was open for 1% of the time, Pallas kernels for 0%

commit v1 on v0

v1 whole, which is shorter than its diff:
```python
import functools
import math

import jax
import jax.numpy as jnp
from jax import lax
from jax.experimental import pallas as pl
from jax.experimental.pallas import tpu as pltpu
from jax.sharding import PartitionSpec as P

MESH = pl.DeviceIdType.MESH
GRID = 256
NZ = 32
NI = 8
NQ = 32
STICK = 8
VALS = 8
VMEM_LIMIT = 60 * 1024 * 1024


def place():
    band = lax.axis_index("band")
    pw = lax.axis_index("pw")
    z = band // NI * 16 + pw // 4
    return z, pw % 4, band % NI


def device(z, y, i):
    return (z // 16 * NI + i, z % 16 * 4 + y)


def parity(z):
    return (z + 24) % NZ // 16


def exchange_kernel(send, out, recv, staged, s1, r1, s2, r2, own):
    z, y, i = place()
    q = y * NI + i

    def near(t):
        return device(z, t // NI, t % NI)

    def far(t):
        return device(t, y, i)

    barrier = pltpu.get_barrier_semaphore()

    @pl.loop(1, NZ)
    def _(p):
        pl.semaphore_signal(barrier, inc=1, device_id=far((z + p) % NZ), device_id_type=MESH)

    @pl.loop(1, NQ)
    def _(p):
        pl.semaphore_signal(barrier, inc=1, device_id=near((q + p) % NQ), device_id_type=MESH)

    pl.semaphore_wait(barrier, NZ + NQ - 2)

    def first(slot_src, slot_dst, sem_send, sem_recv, target):
        return pltpu.make_async_remote_copy(
            src_ref=send.at[slot_src],
            dst_ref=recv.at[slot_dst],
            send_sem=s1.at[sem_send],
            recv_sem=r1.at[sem_recv],
            device_id=target,
            device_id_type=MESH,
        )

    def second(slot_src, slot_dst, sem_send, sem_recv, target):
        return pltpu.make_async_remote_copy(
            src_ref=staged.at[slot_src],
            dst_ref=out.at[slot_dst],
            send_sem=s2.at[sem_send],
            recv_sem=r2.at[sem_recv],
            device_id=target,
            device_id_type=MESH,
        )

    @pl.loop(1, NQ)
    def _(p):
        t = (q + p) % NQ
        first(t, q, t, q, near(t)).start()

    local = pltpu.make_async_copy(send.at[q], recv.at[q], own.at[0])
    local.start()
    local.wait()

    @pl.loop(1, NQ)
    def _(p):
        t = (q + NQ - p) % NQ
        first(t, t, t, t, near(t)).wait_recv()

    turned = jnp.swapaxes(recv[...].astype(jnp.float32), 0, 1)
    low, high = turned[:, :16], turned[:, 16:]
    left = lax.broadcasted_iota(jnp.int32, low.shape, 2) < 64
    staged[0:16] = jnp.where(left, low, pltpu.roll(high, 64, 2)).astype(jnp.bfloat16)
    staged[16:32] = jnp.where(left, pltpu.roll(low, 64, 2), high).astype(jnp.bfloat16)

    @pl.loop(1, NZ)
    def _(p):
        t = (z + (16 + p // 2 * (1 - p % 2 * 2))) % NZ
        second(t, z, t, z, far(t)).start()

    local2 = pltpu.make_async_copy(staged.at[z], out.at[z], own.at[1])
    local2.start()
    local2.wait()

    @pl.loop(1, NZ)
    def _(p):
        t = (z + NZ - p) % NZ
        second(t, t, t, t, far(t)).wait_recv()

    @pl.loop(1, NQ)
    def _(p):
        t = (q + p) % NQ
        first(t, t, t, t, near(t)).wait_send()

    @pl.loop(1, NZ)
    def _(p):
        t = (z + p) % NZ
        second(t, t, t, t, far(t)).wait_send()


def exchange(tiles):
    return pl.pallas_call(
        exchange_kernel,
        out_shape=jax.ShapeDtypeStruct((NZ, 16, 128), jnp.bfloat16),
        in_specs=[pl.BlockSpec(memory_space=pltpu.VMEM)],
        out_specs=pl.BlockSpec(memory_space=pltpu.VMEM),
        scratch_shapes=[
            pltpu.VMEM((NQ, 16, 128), jnp.bfloat16),
            pltpu.VMEM((NZ, 16, 128), jnp.bfloat16),
            pltpu.SemaphoreType.DMA((NQ,)),
            pltpu.SemaphoreType.DMA((NQ,)),
            pltpu.SemaphoreType.DMA((NZ,)),
            pltpu.SemaphoreType.DMA((NZ,)),
            pltpu.SemaphoreType.DMA((2,)),
        ],
        compiler_params=pltpu.CompilerParams(collective_id=1, has_side_effects=True),
        name="exchange",
    )(tiles)


def planes_kernel(scale, weight, vals, xs, ys, table, dens, rows, spread, total, half):
    flat = vals[...].reshape(NZ * 16, 128).astype(jnp.float32).T
    for h in range(2):
        part = flat[h * 64 : h * 64 + 64].reshape(VALS, STICK, NZ * 16)
        rows[:, :, h * 512 : h * 512 + 512] = jnp.swapaxes(part, 0, 1).astype(jnp.bfloat16)
    count = rows.shape[2]

    def gather(s, _):
        grid_at = lax.broadcasted_iota(jnp.int32, (GRID, count), 0)
        hit_x = jnp.where(grid_at == xs[pl.ds(s, 1), :], 1.0, 0.0).astype(jnp.bfloat16)
        hit_y = jnp.where(grid_at == ys[pl.ds(s, 1), :], 1.0, 0.0).astype(jnp.bfloat16)
        value = rows[s]
        for v in range(VALS):
            spread[v * GRID : (v + 1) * GRID, :] = hit_y * value[v : v + 1, :]
        product = lax.dot_general(
            spread[...], hit_x, (((1,), (1,)), ((), ())), preferred_element_type=jnp.float32
        )

        @pl.when(s == 0)
        def _():
            total[...] = product

        @pl.when(s != 0)
        def _():
            total[...] += product

        return 0

    lax.fori_loop(0, STICK, gather, 0)
    for b in range(4):
        real = total[b * GRID : (b + 1) * GRID, :]
        imag = total[(4 + b) * GRID : (5 + b) * GRID, :]
        plane = jnp.concatenate([real, imag], 0).astype(jnp.bfloat16)
        mid = jnp.dot(table[...], plane, preferred_element_type=jnp.float32).astype(jnp.bfloat16)
        half[:, 0:GRID] = mid[0:GRID]
        half[:, GRID : 2 * GRID] = mid[GRID : 2 * GRID]
        wave = lax.dot_general(
            table[...], half[...], (((1,), (1,)), ((), ())), preferred_element_type=jnp.float32
        )
        power = wave[0:GRID] * wave[0:GRID] + wave[GRID:] * wave[GRID:]
        term = power * (weight[b].astype(jnp.float32) * scale)
        if b == 0:
            dens[...] = term
        else:
            dens[...] += term


def planes(weight, vals, xs, ys, table, scale):
    vmem = pl.BlockSpec(memory_space=pltpu.VMEM)
    return pl.pallas_call(
        functools.partial(planes_kernel, scale),
        out_shape=jax.ShapeDtypeStruct((GRID, GRID), jnp.float32),
        in_specs=[pl.BlockSpec(memory_space=pltpu.SMEM)] + [vmem] * 4,
        out_specs=vmem,
        scratch_shapes=[
            pltpu.VMEM((STICK, VALS, NZ * NQ), jnp.bfloat16),
            pltpu.VMEM((VALS * GRID, NZ * NQ), jnp.bfloat16),
            pltpu.VMEM((VALS * GRID, GRID), jnp.float32),
            pltpu.VMEM((GRID, 2 * GRID), jnp.bfloat16),
        ],
        compiler_params=pltpu.CompilerParams(vmem_limit_bytes=VMEM_LIMIT),
        name="planes",
    )(weight, vals, xs, ys, table)


def collect_kernel(part, out, shares, mine, held, full, s1, r1, s2, r2, s3, r3):
    z, y, i = place()
    slot = parity(z)
    up, down = (z + 8) % NZ, (z + 24) % NZ
    barrier = pltpu.get_barrier_semaphore()
    for t in (up, down):
        pl.semaphore_signal(barrier, inc=1, device_id=device(t, y, i), device_id_type=MESH)

    @pl.loop(1, NI)
    def _(p):
        pl.semaphore_signal(
            barrier, inc=1, device_id=device(z, y, (i + p) % NI), device_id_type=MESH
        )

    pl.semaphore_wait(barrier, NI + 1)

    def share(src, dst, t):
        return pltpu.make_async_remote_copy(
            src_ref=part.at[src],
            dst_ref=shares.at[dst],
            send_sem=s1.at[src],
            recv_sem=r1.at[dst],
            device_id=device(z, y, t),
            device_id_type=MESH,
        )

    @pl.loop(1, NI)
    def _(p):
        t = (i + p) % NI
        share(t, i, t).start()

    @pl.loop(1, NI)
    def _(p):
        t = (i + NI - p) % NI
        share(t, t, t).wait_recv()

    shares[i] = part[i]
    total = shares[0]
    for t in range(1, NI):
        total = total + shares[t]
    mine[...] = total.astype(jnp.bfloat16)

    def hop(which, at, t):
        return pltpu.make_async_remote_copy(
            src_ref=mine,
            dst_ref=held.at[at],
            send_sem=s2.at[which],
            recv_sem=r2.at[at],
            device_id=device(t, y, i),
            device_id_type=MESH,
        )

    hop(0, slot, up).start()
    hop(1, slot, down).start()

    def spread(k, src, t):
        return pltpu.make_async_remote_copy(
            src_ref=held.at[k],
            dst_ref=full.at[k, src],
            send_sem=s3.at[k, t],
            recv_sem=r3.at[k, src],
            device_id=device(z, y, t),
            device_id_type=MESH,
        )

    for k in range(2):
        hop(0, k, up).wait_recv()

        @pl.loop(1, NI)
        def _(p):
            t = (i + p) % NI
            spread(k, i, t).start()

        out[k, i] = held[k].astype(jnp.float32)

    for k in range(2):

        @pl.loop(1, NI)
        def _(p):
            t = (i + NI - p) % NI
            spread(k, t, t).wait_recv()
            out[k, t] = full[k, t].astype(jnp.float32)

    hop(0, slot, up).wait_send()
    hop(1, slot, down).wait_send()

    @pl.loop(1, NI)
    def _(p):
        t = (i + p) % NI
        share(t, t, t).wait_send()
        for k in range(2):
            spread(k, t, t).wait_send()


def collect(part):
    height = GRID // NI
    vmem = pl.BlockSpec(memory_space=pltpu.VMEM)
    dma = pltpu.SemaphoreType.DMA
    result = pl.pallas_call(
        collect_kernel,
        out_shape=jax.ShapeDtypeStruct((2, NI, height, GRID), jnp.float32),
        in_specs=[vmem],
        out_specs=vmem,
        scratch_shapes=[
            pltpu.VMEM((NI, height, GRID), jnp.float32),
            pltpu.VMEM((height, GRID), jnp.bfloat16),
            pltpu.VMEM((2, height, GRID), jnp.bfloat16),
            pltpu.VMEM((2, NI, height, GRID), jnp.bfloat16),
            dma((NI,)),
            dma((NI,)),
            dma((2,)),
            dma((2,)),
            dma((2, NI)),
            dma((2, NI)),
        ],
        compiler_params=pltpu.CompilerParams(collective_id=2, has_side_effects=True),
        name="collect",
    )(part.reshape(NI, height, GRID))
    return result.reshape(2, GRID, GRID)


def angles(product):
    return 2.0 * math.pi / GRID * (product % GRID).astype(jnp.float32)


def transform(coeffs, rotation_matrix, lengths, planes_at):
    real, imag = rotation_matrix[0], rotation_matrix[1]
    to_real = jnp.concatenate([real, -imag], 0).T
    to_imag = jnp.concatenate([imag, real], 0).T
    forms = jnp.stack([to_real, -to_imag, to_imag, to_real, -to_imag, -to_real, to_real, -to_imag])
    forms = forms.reshape(2, 2, 2, 2, NI, 2, 128)
    forms = jnp.transpose(forms, (0, 4, 1, 3, 5, 2, 6))
    rotated = jnp.einsum(
        "ok,ksj->osj",
        forms.reshape(2 * NI * VALS * 2, 128),
        coeffs.reshape(128, STICK, GRID),
        preferred_element_type=jnp.float32,
    ).astype(jnp.bfloat16)
    at = jnp.arange(GRID, dtype=jnp.int32)
    live = (at[None, :] < lengths[:, None]).astype(jnp.bfloat16)
    masked = (rotated * live).reshape(2, NI * VALS, 2, STICK, GRID)
    turn = angles(planes_at[:, None] * at[None, :])
    waves = jnp.stack([jnp.cos(turn), jnp.sin(turn)], 1).astype(jnp.bfloat16)
    amplitude = jnp.einsum("ktj,gntsj->gkns", waves, masked, preferred_element_type=jnp.float32)
    phase = -angles(planes_at[:, None] * (lengths // 2)[None, :])[:, None, :]
    values = amplitude[0] * jnp.cos(phase) + amplitude[1] * jnp.sin(phase)
    values = values.astype(jnp.bfloat16).reshape(2, 4, 16, NI, VALS * STICK)
    return jnp.transpose(values, (1, 3, 2, 0, 4)).reshape(NQ, 16, 128)


def shards(coeffs, rotation_matrix, stick_length, stick_column, plane_index, occupation):
    band_count = lax.axis_size("band")
    z, y, i = place()
    row = lax.axis_index("band") * lax.axis_size("pw") + lax.axis_index("pw")
    lengths = lax.dynamic_slice_in_dim(stick_length, row * STICK, STICK)
    by_group = plane_index.reshape(16, 4, 2)
    lower, upper = by_group[0:8], by_group[8:16]
    ordered = jnp.stack(
        [
            jnp.concatenate([upper[:, :, 1], lower[:, :, 0]], 0).T,
            jnp.concatenate([upper[:, :, 0], lower[:, :, 1]], 0).T,
        ]
    )
    tiles = transform(coeffs, rotation_matrix, lengths, ordered.reshape(-1))
    received = exchange(tiles)
    column = jnp.transpose(stick_column.reshape(2, NI, 16, 2, 2, STICK), (3, 5, 0, 2, 4, 1))
    column = jnp.transpose(column.reshape(2, STICK, 512), (1, 0, 2)).reshape(STICK, 1024)
    pair = [(b, (b + NI) % band_count) for b in range(band_count)]
    other = lax.ppermute(occupation, "band", pair)
    low = z < 16
    weight = jnp.concatenate(
        [jnp.where(low, occupation, other), jnp.where(low, other, occupation)]
    )
    at = jnp.arange(GRID, dtype=jnp.int32)
    turn = angles(at[:, None] * at[None, :])
    cos_table = jnp.cos(turn).astype(jnp.bfloat16)
    sin_table = jnp.sin(turn).astype(jnp.bfloat16)
    table = jnp.concatenate(
        [
            jnp.concatenate([cos_table, -sin_table], 1),
            jnp.concatenate([sin_table, cos_table], 1),
        ],
        0,
    )
    scale = 1.0 / float(occupation.shape[0] * band_count * stick_column.shape[0] * GRID)
    part = planes(weight, received, column // GRID, column % GRID, table, scale)
    return collect(part)


def solution(mesh):
    return jax.shard_map(
        shards,
        mesh=mesh,
        in_specs=(P(None, None, ("band", "pw"), None), P(), P(), P(), P(), P("band")),
        out_specs=P("pw", None, None),
        check_vma=False,
    )
```

time: 783 us -> 140 us (0.18)
  waiting for transfers between devices: 444 us -> 0.01 us
  local copies, waits for them, and re-layouts: 220 us -> 19.1 us
  Pallas kernels: 0 us -> 78.6 us
  matrix products: 37.4 us -> 0.86 us
  starting transfers between devices: 61.8 us -> 29.6 us
  between operations: 13.6 us -> 0.25 us
    psum x1 -> x0, waiting for transfers between devices: 401 us -> none  [shards(): return lax.psum(local_sum, 'band')]
    scatter x4 -> x0, local copies, waits for them, and re-layouts: 121 us -> none  [one_plane(): jnp.zeros((2, grid_len * grid_len), jnp.bfloat16).at[:, columns]]
    slice x4 -> x10, local copies, waits for them, and re-layouts: 86 us -> 0.91 us  [the longest x3 0.3 us: shards(): lower, upper = (by_group[0:8], by_group[8:16])]
    pallas_call x0 -> x3, Pallas kernels: none -> 78.6 us  [the longest x1 34.2 us: exchange(): pl.pallas_call(exchange_kernel, out_shape=jax.ShapeDtypeStruct((NZ, 16, 1...]
    all_to_all x2 -> x0, starting transfers between devices: 61.8 us -> none  [the longest x1 32.3 us: shards(): lax.all_to_all(rotated, 'band', split_axis=1, concat_axis=2, tiled=True)]
    all_to_all x2 -> x0, waiting for transfers between devices: 42.9 us -> none  [the longest x1 22.2 us: shards(): lax.all_to_all(rotated, 'band', split_axis=1, concat_axis=2, tiled=True)]
    dot_general x35 -> x2, matrix products: 37.4 us -> 0.86 us  [the longest x1 0.44 us: transform(): jnp.einsum('ktj,gntsj->gkns', waves, masked, preferred_element_type=jnp.f...]
    ppermute x0 -> x1, starting transfers between devices: none -> 29.6 us  [shards(): other = lax.ppermute(occupation, 'band', pair)]
  transfers between devices with their start and end apart: 3 -> 1, of which waited for: 3 -> 0; matrix products, arithmetic and copies ran while one was open for 1% -> 21% of each run, Pallas kernels for 0% -> 24%
where the time goes in v1:
time: 140 us
  Pallas kernels  78.6 us (56%)
  starting transfers between devices  29.6 us (21%)
  local copies, waits for them, and re-layouts  19.1 us (14%)
  other arithmetic  11.6 us (8%)
    pallas_call x1, Pallas kernels, exchange(): pl.pallas_call(exchange_kernel, out_shape=jax.ShapeDtypeStruct((NZ, 16, 1...  34.2 us
    ppermute x1, starting transfers between devices, shards(): other = lax.ppermute(occupation, 'band', pair)  29.6 us
    pallas_call x1, Pallas kernels, collect(): pl.pallas_call(collect_kernel, out_shape=jax.ShapeDtypeStruct((2, NI, hei...  28.7 us
    pallas_call x1, Pallas kernels, planes(): pl.pallas_call(functools.partial(planes_kernel, scale), out_shape=jax.Sha...  15.6 us
    mul x4, local copies, waits for them, and re-layouts, transform(): values = amplitude[0] * jnp.cos(phase) + amplitude[1] * jnp.sin(phase)  5.56 us
    transpose x1, other arithmetic, transform(): return jnp.transpose(values, (1, 3, 2, 0, 4)).reshape(NQ, 16, 128)  4.78 us
    squeeze x2, local copies, waits for them, and re-layouts, transform(): values = amplitude[0] * jnp.cos(phase) + amplitude[1] * jnp.sin(phase)  4.13 us
  transfers between devices with their start and end apart: 1, of which 0 were waited for; matrix products, arithmetic and copies ran while one was open for 21% of the time, Pallas kernels for 24%

profile of v1, /device:TPU:1, one launch (start us, length us, event | category | flops | bytes accessed | tf_op | source)
XLA Modules:
  0.0 139.9 jit_solution(11837263665444801008)
XLA Ops:
  0.0 29.6 %collective-permute-start = (s32[2]{0:T(128)}, s32[2]{0:T(128)S(1)}, u32[]{:S(2)}, u32[]{:S(2)}) collective-permute-start(s32[2]{0:T(128)} %param.11), channel_id=1, source_target_pairs={{0,512},{64,576},{128,640},{192,704},{256,768},{320,832},{384,896}... | collective-permute-start | bytes 32 | tf_op jit(solution)/shard_map/ppermute | solution.py:376
  29.7 0.7 fusion.28
  30.4 0.7 slice_bitcast_fusion
  31.1 1.1 sine_convert_fusion
  32.2 1.0 fusion.17
  33.5 0.8 and_select_fusion
  34.4 0.4 fusion
  34.8 0.6 copy.27
  35.5 0.1 slice.58
  35.7 0.1 copy.19
  35.8 0.1 slice.55
  36.0 0.1 copy.18
  36.5 0.6 cosine_convert_fusion.1
  37.1 0.4 convolution_bitcast_fusion
  37.6 1.4 %squeeze.31 = f32[2,4,16,8,64]{2,1,0,4,3:T(4,128)S(1)} reshape(f32[1,128,64,8]{1,3,2,0:T(8,128)S(1)} %get-tuple-element.12) | data formatting | bytes 524288 | tf_op jit(solution)/shard_map/squeeze | solution.py:353
  39.0 0.1 fusion.26
  39.1 2.7 %mul.178 = f32[2,4,16,8,64]{2,1,0,4,3:T(4,128)} reshape(f32[128,64,8]{0,2,1:T(8,128)S(1)} %mul.177) | data formatting | bytes 524288 | tf_op jit(solution)/shard_map/mul | solution.py:353
  41.9 2.7 %squeeze.30 = f32[2,4,16,8,64]{2,1,0,4,3:T(4,128)} reshape(f32[1,128,64,8]{1,3,2,0:T(8,128)S(1)} %get-tuple-element.11) | data formatting | bytes 524288 | tf_op jit(solution)/shard_map/squeeze | solution.py:353
  44.6 2.8 %mul.175 = f32[2,4,16,8,64]{2,1,0,4,3:T(4,128)} reshape(f32[128,64,8]{0,2,1:T(8,128)S(1)} %mul.174) | data formatting | bytes 524288 | tf_op jit(solution)/shard_map/mul | solution.py:353
  47.4 4.8 %fusion.1 = bf16[4,8,16,2,64]{2,0,3,4,1:T(4,128)(2,1)} fusion(f32[2,4,16,8,64]{2,1,0,4,3:T(4,128)S(1)} %squeeze.31, f32[2,4,16,8,64]{2,1,0,4,3:T(4,128)} %mul.178, f32[2,4,16,8,64]{2,1,0,4,3:T(4,128)} %squeeze.30, f32[2,4,16,8,64]{2,1,0,4,3:T(4,128)} %mul.175), kind=kLoop, calls=%fused_computation.4 | loop fusion | flops 262144 | bytes 1179648 | tf_op jit(solution)/shard_map/transpose | solution.py:355
  52.2 1.8 %copy.23 = bf16[4,8,16,2,64]{4,3,2,1,0:T(2,128)(2,1)S(1)} copy(bf16[4,8,16,2,64]{2,0,3,4,1:T(4,128)(2,1)} %fusion.1) | data formatting | bytes 262144 | tf_op jit(solution)/shard_map/transpose | solution.py:355
  54.0 0.8 reshape.257.send
  54.8 34.2 %exchange.1.vals = bf16[32,16,128]{2,1,0:T(8,128)(2,1)} custom-call(bf16[32,16,128]{2,1,0:T(8,128)(2,1)} %reshape.257.send), custom_call_target="tpu_custom_call" | custom-call | tf_op jit(solution)/shard_map/exchange/pallas_call | solution.py:124
  89.0 0.8 reshape.258
  89.9 1.0 copy.24
  90.8 0.7 reshape.259
  91.6 0.7 add_select_fusion.2
  92.2 0.8 maximum_maximum_fusion.table
  93.1 0.6 pad_add_fusion.1.weight
  93.7 15.6 %planes.1 = f32[256,256]{1,0:T(8,128)} custom-call(s32[4]{0:T(128)} %pad_add_fusion.1.weight, bf16[32,16,128]{2,1,0:T(8,128)(2,1)} %exchange.1.vals, s32[8,1024]{1,0:T(8,128)} %get-tuple-element.14.xs, s32[8,1024]{1,0:T(8,128)} %get-tuple-element.13.ys, bf16[512,512]{1,0:T(8,128)(2,1)} %maximum_maximum_fusion.table), custom_call_target="tpu_custom_call" | custom-call | tf_op jit(solution)/shard_map/planes/pallas_call | solution.py:192
  109.3 28.7 %collect.1 = f32[2,8,32,256]{3,2,1,0:T(8,128)} custom-call(f32[8,32,256]{2,1,0:T(8,128)} %bitcast.88), custom_call_target="tpu_custom_call" | custom-call | tf_op jit(solution)/shard_map/collect/pallas_call | solution.py:306
  138.1 1.9 %copy.38 = f32[2,256,256]{2,1,0:T(8,128)} copy(f32[2,256,256]{2,1,0:T(8,128)} %bitcast.86) | data formatting | bytes 1048576
  (31 shorter events, 1.1 us)
Async XLA Ops:
  0.0 34.4 %copy-start = (bf16[2,64,8,256]{3,2,1,0:T(8,128)(2,1)S(1)}, bf16[2,64,8,256]{3,2,1,0:T(8,128)(2,1)}, u32[]{:S(2)}) copy-start(bf16[2,64,8,256]{3,2,1,0:T(8,128)(2,1)} %param.6) | copy-start | bytes 1572868
  0.0 93.1 %collective-permute-start = (s32[2]{0:T(128)}, s32[2]{0:T(128)S(1)}, u32[]{:S(2)}, u32[]{:S(2)}) collective-permute-start(s32[2]{0:T(128)} %param.11), channel_id=1, source_target_pairs={{0,512},{64,576},{128,640},{192,704},{256,768},{320,832},{384,896}... | collective-permute-start | bytes 32 | tf_op jit(solution)/shard_map/ppermute | solution.py:376
  32.2 3.2 %copy-start.2 = (s32[128]{0:T(128)S(1)}, s32[128]{0:T(128)}, u32[]{:S(2)}) copy-start(s32[128]{0:T(128)} %param.10) | copy-start | bytes 1540
  47.4 41.6 %copy-start.1 = (s32[8192]{0:T(1024)S(1)}, s32[8192]{0:T(1024)}, u32[]{:S(2)}) copy-start(s32[8192]{0:T(1024)} %param.9) | copy-start | bytes 98308
  54.0 39.1 %copy-start.3 = (s32[2]{0:T(128)S(1)}, s32[2]{0:T(128)}, u32[]{:S(2)}) copy-start(s32[2]{0:T(128)} %param.11) | copy-start | bytes 28

commit v2 on v0

v2 whole, which is shorter than its diff:
```python
import math

import jax
import jax.numpy as jnp
import numpy as np
from jax import lax
from jax.experimental import pallas as pl
from jax.experimental.pallas import tpu as pltpu
from jax.sharding import PartitionSpec as P

MESH = pl.DeviceIdType.MESH
GRID = 256
NZ = 32
NI = 8
NQ = 32
STICK = 8
VALS = 8
OCTET = 8 * 16 * 16
HIGH = GRID // NI
VMEM_LIMIT = 62 * 1024 * 1024
ACROSS = (((1,), (1,)), ((), ()))


def place():
    band = lax.axis_index("band")
    pw = lax.axis_index("pw")
    z = band // NI * 16 + pw // 4
    return z, pw % 4, band % NI


def device(z, y, i):
    return (z // 16 * NI + i, z % 16 * 4 + y)


def parity(z):
    return (z + 24) % NZ // 16


def fourier():
    at = np.arange(GRID)
    turn = np.float32(2.0 * math.pi / GRID) * (at[:, None] * at[None, :] % GRID).astype(np.float32)
    cos, sin = np.cos(turn), np.sin(turn)
    return np.concatenate([np.concatenate([cos, -sin], 1), np.concatenate([sin, cos], 1)], 0)


def band_choice():
    choice = np.zeros((2, NI, 2, 4, 2, 32), np.float32)
    for i in range(NI):
        for k in range(4):
            b = k // 2 * 16 + 2 * i + k % 2
            choice[0, i, 0, k, 0, b] = 1.0
            choice[0, i, 1, k, 1, b] = 1.0
            choice[1, i, 0, k, 1, b] = 1.0
            choice[1, i, 1, k, 0, b] = -1.0
    return choice.reshape(128, 64)


def plane_order():
    order = np.zeros((2, 4, 16, 128), np.float32)
    for high in range(2):
        for y in range(4):
            for low in range(16):
                k = 2 * ((low + 8) % 16 * 4 + y) + parity(high * 16 + low)
                order[high, y, low, k] = 1.0
    return order.reshape(128, 128)


def dot(a, b):
    return jnp.dot(a, b, preferred_element_type=jnp.float32)


def dot_across(a, b):
    return lax.dot_general(a, b, ACROSS, preferred_element_type=jnp.float32)


def narrow(a):
    return a.astype(jnp.bfloat16)


def wide(a):
    return a.astype(jnp.float32)


def kernel(
    scale,
    coeffs,
    rotation,
    live,
    phase,
    picked,
    xs,
    ys,
    share_own,
    table,
    choice,
    order,
    out,
    send,
    recv,
    staged,
    sticks,
    turned,
    spread,
    hits,
    total,
    half,
    part,
    shares,
    mine,
    held,
    share_other,
    s1,
    r1,
    s2,
    r2,
    s3,
    r3,
    s4,
    r4,
    s5,
    r5,
    own,
    s6,
    r6,
):
    z, y, i = place()
    q = y * NI + i

    def near(t):
        return device(z, t // NI, t % NI)

    def far(t):
        return device(t, y, i)

    barrier = pltpu.get_barrier_semaphore()

    @pl.loop(1, NZ)
    def _(p):
        pl.semaphore_signal(barrier, inc=1, device_id=far((z + p) % NZ), device_id_type=MESH)

    @pl.loop(1, NQ)
    def _(p):
        pl.semaphore_signal(barrier, inc=1, device_id=near((q + p) % NQ), device_id_type=MESH)

    by_stick = narrow(jnp.swapaxes(wide(coeffs[...]), 0, 1))
    forms = narrow(dot_across(choice[...], rotation[...]))
    for s in range(STICK):
        rotated = wide(narrow(dot(forms, by_stick[s])) * live[s : s + 1, :])
        for t in range(2):
            turned[:, s, :, t * GRID : (t + 1) * GRID] = rotated[t * 64 : t * 64 + 64].reshape(
                NI, VALS, GRID
            )
    rows = narrow(turned[...].reshape(NI * STICK * VALS, 2 * GRID))
    waves0 = narrow(dot(picked[...], table[0:GRID, :]))
    waves1 = narrow(dot(picked[...], table[GRID : 2 * GRID, :]))
    cos = jnp.concatenate([phase[0]] * 4, 1)
    sin = jnp.concatenate([phase[1]] * 4, 1)
    values = dot_across(waves0, rows) * cos + dot_across(waves1, rows) * sin
    values = dot(order[...], narrow(values))
    left = lax.broadcasted_iota(jnp.int32, (16, 128), 1) < 64
    for b in range(4):
        for pair in range(4):
            lower = values[b * 16 : b * 16 + 16, pair * 128 : pair * 128 + 128]
            upper = values[64 + b * 16 : 80 + b * 16, pair * 128 : pair * 128 + 128]
            at = b * NI + 2 * pair
            send[at] = narrow(jnp.where(left, lower, pltpu.roll(upper, 64, 1)))
            send[at + 1] = narrow(jnp.where(left, pltpu.roll(lower, 64, 1), upper))

    pl.semaphore_wait(barrier, NZ + NQ - 2)

    def first(slot_src, slot_dst, target):
        return pltpu.make_async_remote_copy(
            src_ref=send.at[slot_src],
            dst_ref=recv.at[slot_dst],
            send_sem=s1.at[slot_src],
            recv_sem=r1.at[slot_dst],
            device_id=target,
            device_id_type=MESH,
        )

    def second(slot_src, slot_dst, target):
        return pltpu.make_async_remote_copy(
            src_ref=staged.at[slot_src],
            dst_ref=sticks.at[slot_dst],
            send_sem=s2.at[slot_src],
            recv_sem=r2.at[slot_dst],
            device_id=target,
            device_id_type=MESH,
        )

    @pl.loop(1, NQ)
    def _(p):
        t = (q + p) % NQ
        first(t, q, near(t)).start()

    weights = pltpu.make_async_remote_copy(
        src_ref=share_own,
        dst_ref=share_other,
        send_sem=s6,
        recv_sem=r6,
        device_id=far((z + 16) % NZ),
        device_id_type=MESH,
    )
    weights.start()
    keep = pltpu.make_async_copy(send.at[q], recv.at[q], own.at[0])
    keep.start()
    keep.wait()

    @pl.loop(1, NQ)
    def _(p):
        t = (q + NQ - p) % NQ
        first(t, t, near(t)).wait_recv()

    swapped = jnp.swapaxes(wide(recv[...]), 0, 1)
    lower, upper = swapped[:, :16], swapped[:, 16:]
    left = lax.broadcasted_iota(jnp.int32, lower.shape, 2) < 64
    staged[0:16] = narrow(jnp.where(left, lower, pltpu.roll(upper, 64, 2)))
    staged[16:32] = narrow(jnp.where(left, pltpu.roll(lower, 64, 2), upper))

    @pl.loop(1, NZ)
    def _(p):
        t = (z + (16 + p // 2 * (1 - p % 2 * 2))) % NZ
        second(t, z, far(t)).start()

    keep2 = pltpu.make_async_copy(staged.at[z], sticks.at[z], own.at[1])
    keep2.start()
    keep2.wait()

    @pl.loop(0, 4)
    def _(step):
        octet = (z // 8 + step + step // 2 - 2 * (step // 3)) % 4

        @pl.loop(0, 8)
        def _(p):
            t = octet * 8 + p

            @pl.when(t != z)
            def _():
                second(t, t, far(t)).wait_recv()

        block = wide(sticks[pl.ds(octet * 8, 8)].reshape(128, 128)).T
        held_rows = block.reshape(16, VALS, 128)
        shares_rows = narrow(held_rows)
        for b in range(16):
            grid_at = lax.broadcasted_iota(jnp.int32, (GRID, 128), 0)
            hit_x = narrow(jnp.where(grid_at == xs[octet, b : b + 1, :], 1.0, 0.0))
            hit_y = narrow(jnp.where(grid_at == ys[octet, b : b + 1, :], 1.0, 0.0))
            hits[:, b * 128 : b * 128 + 128] = hit_x
            for v in range(VALS):
                spread[v * GRID : (v + 1) * GRID, b * 128 : b * 128 + 128] = (
                    hit_y * shares_rows[b, v : v + 1, :]
                )

        @pl.loop(0, 4)
        def _(m):
            at = pl.ds(pl.multiple_of(m * 512, 512), 512)
            product = dot_across(spread[at, :], hits[...])

            @pl.when(step == 0)
            def _():
                total[at, :] = product

            @pl.when(step != 0)
            def _():
                total[at, :] += product

    weights.wait_recv()
    low = z < 16
    for b in range(4):
        real = total[b * GRID : (b + 1) * GRID, :]
        imag = total[(4 + b) * GRID : (5 + b) * GRID, :]
        mid = narrow(dot(table[...], narrow(jnp.concatenate([real, imag], 0))))
        half[:, 0:GRID] = mid[0:GRID]
        half[:, GRID : 2 * GRID] = mid[GRID : 2 * GRID]
        wave = dot_across(table[...], half[...])
        power = wave[0:GRID] * wave[0:GRID] + wave[GRID:] * wave[GRID:]
        here, there = share_own[b % 2, 0:1, :], share_other[b % 2, 0:1, :]
        weight = jnp.where(low, here, there) if b < 2 else jnp.where(low, there, here)
        term = power * (jnp.concatenate([weight, weight], 1) * scale)
        term = term.reshape(NI, HIGH, GRID)
        if b == 0:
            part[...] = term
        else:
            part[...] += term

    def share(src, dst, t):
        return pltpu.make_async_remote_copy(
            src_ref=part.at[src],
            dst_ref=shares.at[dst],
            send_sem=s3.at[src],
            recv_sem=r3.at[dst],
            device_id=device(z, y, t),
            device_id_type=MESH,
        )

    @pl.loop(1, NI)
    def _(p):
        t = (i + p) % NI
        share(t, i, t).start()

    shares[i] = part[i]

    @pl.loop(1, NI)
    def _(p):
        t = (i + NI - p) % NI
        share(t, t, t).wait_recv()

    summed = shares[0]
    for t in range(1, NI):
        summed = summed + shares[t]
    mine[...] = narrow(summed)
    slot = parity(z)
    up, down = (z + 8) % NZ, (z + 24) % NZ

    def hop(which, at, t):
        return pltpu.make_async_remote_copy(
            src_ref=mine,
            dst_ref=held.at[at],
            send_sem=s4.at[which],
            recv_sem=r4.at[at],
            device_id=far(t),
            device_id_type=MESH,
        )

    hop(0, slot, up).start()
    hop(1, slot, down).start()

    def spread_out(k, src, t):
        return pltpu.make_async_remote_copy(
            src_ref=held.at[k],
            dst_ref=out.at[k, src],
            send_sem=s5.at[k, t],
            recv_sem=r5.at[k, src],
            device_id=device(z, y, t),
            device_id_type=MESH,
        )

    for k in range(2):
        hop(0, k, up).wait_recv()

        @pl.loop(1, NI)
        def _(p):
            t = (i + p) % NI
            spread_out(k, i, t).start()

        out[k, i] = held[k]

    for k in range(2):

        @pl.loop(1, NI)
        def _(p):
            t = (i + NI - p) % NI
            spread_out(k, t, t).wait_recv()

    weights.wait_send()
    hop(0, slot, up).wait_send()
    hop(1, slot, down).wait_send()

    @pl.loop(1, NI)
    def _(p):
        t = (i + p) % NI
        share(t, t, t).wait_send()
        for k in range(2):
            spread_out(k, t, t).wait_send()

    @pl.loop(1, NQ)
    def _(p):
        t = (q + p) % NQ
        first(t, t, near(t)).wait_send()

    @pl.loop(1, NZ)
    def _(p):
        t = (z + p) % NZ
        second(t, t, far(t)).wait_send()


def shards(coeffs, rotation_matrix, stick_length, stick_column, plane_index, occupation):
    band_count = lax.axis_size("band")
    row = lax.axis_index("band") * lax.axis_size("pw") + lax.axis_index("pw")
    lengths = lax.dynamic_slice_in_dim(stick_length, row * STICK, STICK)
    real, imag = rotation_matrix[0], rotation_matrix[1]
    rotation = jnp.concatenate(
        [jnp.concatenate([real, imag], 1), jnp.concatenate([-imag, real], 1)], 0
    )
    at = jnp.arange(GRID, dtype=jnp.int32)
    live = narrow(at[None, :] < lengths[:, None])
    shift = jnp.broadcast_to((lengths // 2)[None, :, None], (2, STICK, VALS)).reshape(1, 128)
    product = plane_index[:, None] * shift % GRID
    angle = 2.0 * math.pi / GRID * wide(product)
    phase = jnp.stack([jnp.cos(angle), jnp.sin(angle)])
    picked = narrow(plane_index[:, None] == at[None, :])
    column = stick_column.reshape(2, NI, 2, 8, 2, 2, STICK)
    column = jnp.transpose(column, (0, 2, 4, 6, 3, 5, 1)).reshape(4, 16, 128)
    weights = jnp.broadcast_to(wide(occupation)[:, None, None], (2, 8, 128))
    scale = 1.0 / float(occupation.shape[0] * band_count * stick_column.shape[0] * GRID)
    vmem = pl.BlockSpec(memory_space=pltpu.VMEM)
    dma = pltpu.SemaphoreType.DMA
    bf16, f32 = jnp.bfloat16, jnp.float32
    result = pl.pallas_call(
        lambda *refs: kernel(scale, *refs),
        out_shape=jax.ShapeDtypeStruct((2, NI, HIGH, GRID), bf16),
        in_specs=[vmem] * 11,
        out_specs=vmem,
        scratch_shapes=[
            pltpu.VMEM((NQ, 16, 128), bf16),
            pltpu.VMEM((NQ, 16, 128), bf16),
            pltpu.VMEM((NZ, 16, 128), bf16),
            pltpu.VMEM((NZ, 16, 128), bf16),
            pltpu.VMEM((NI, STICK, VALS, 2 * GRID), f32),
            pltpu.VMEM((VALS * GRID, OCTET), bf16),
            pltpu.VMEM((GRID, OCTET), bf16),
            pltpu.VMEM((VALS * GRID, GRID), f32),
            pltpu.VMEM((GRID, 2 * GRID), bf16),
            pltpu.VMEM((NI, HIGH, GRID), f32),
            pltpu.VMEM((NI, HIGH, GRID), f32),
            pltpu.VMEM((HIGH, GRID), bf16),
            pltpu.VMEM((2, HIGH, GRID), bf16),
            pltpu.VMEM((2, 8, 128), f32),
            dma((NQ,)),
            dma((NQ,)),
            dma((NZ,)),
            dma((NZ,)),
            dma((NI,)),
            dma((NI,)),
            dma((2,)),
            dma((2,)),
            dma((2, NI)),
            dma((2, NI)),
            dma((2,)),
            dma,
            dma,
        ],
        compiler_params=pltpu.CompilerParams(
            collective_id=1, has_side_effects=True, vmem_limit_bytes=VMEM_LIMIT
        ),
        name="density",
    )(
        coeffs.reshape(128, STICK, GRID),
        rotation,
        live,
        phase,
        picked,
        column // GRID,
        column % GRID,
        weights,
        jnp.asarray(fourier(), bf16),
        jnp.asarray(band_choice(), bf16),
        jnp.asarray(plane_order(), bf16),
    )
    return wide(result.reshape(2, GRID, GRID))


def solution(mesh):
    return jax.shard_map(
        shards,
        mesh=mesh,
        in_specs=(P(None, None, ("band", "pw"), None), P(), P(), P(), P(), P("band")),
        out_specs=P("pw", None, None),
        check_vma=False,
    )
```

time: 783 us -> 108 us (0.14)
  waiting for transfers between devices: 444 us -> 0 us
  local copies, waits for them, and re-layouts: 220 us -> 3.8 us
  Pallas kernels: 0 us -> 97.2 us
  starting transfers between devices: 61.8 us -> 0 us
  matrix products: 37.4 us -> 0 us
  between operations: 13.6 us -> 0.06 us
    psum x1 -> x0, waiting for transfers between devices: 401 us -> none  [shards(): return lax.psum(local_sum, 'band')]
    scatter x4 -> x0, local copies, waits for them, and re-layouts: 121 us -> none  [one_plane(): jnp.zeros((2, grid_len * grid_len), jnp.bfloat16).at[:, columns]]
    pallas_call x0 -> x1, Pallas kernels: none -> 97.2 us  [shards(): pl.pallas_call(lambda *refs: kernel(scale, *refs), out_shape=jax.ShapeDty...]
    slice x4 -> x1, local copies, waits for them, and re-layouts: 86 us -> 0.01 us  [shards(): real, imag = (rotation_matrix[0], rotation_matrix[1])]
    all_to_all x2 -> x0, starting transfers between devices: 61.8 us -> none  [the longest x1 32.3 us: shards(): lax.all_to_all(rotated, 'band', split_axis=1, concat_axis=2, tiled=True)]
    all_to_all x2 -> x0, waiting for transfers between devices: 42.9 us -> none  [the longest x1 22.2 us: shards(): lax.all_to_all(rotated, 'band', split_axis=1, concat_axis=2, tiled=True)]
    dot_general x35 -> x0, matrix products: 37.4 us -> none  [the longest x33 36.4 us: contract(): return jnp.einsum(form, left, right, preferred_element_type=jnp.float32)]
  transfers between devices with their start and end apart: 3 -> 0, of which waited for: 3 -> 0; matrix products, arithmetic and copies ran while one was open for 1% -> 0% of each run, Pallas kernels for 0% -> 0%
where the time goes in v2:
time: 108 us; the launch traced here: 107 us
  Pallas kernels  97.2 us (90%)
  other arithmetic  6.25 us (6%)
  local copies, waits for them, and re-layouts  3.8 us (4%)
    pallas_call x1, Pallas kernels, shards(): pl.pallas_call(lambda *refs: kernel(scale, *refs), out_shape=jax.ShapeDty...  97.2 us

profile of v2, /device:TPU:1, one launch (start us, length us, event | category | flops | bytes accessed | tf_op | source)
XLA Modules:
  0.0 107.3 jit_solution(11217409808902204475)
XLA Ops:
  0.0 0.8 and_select_fusion
  0.8 0.1 broadcast_in_dim.4
  0.8 0.0 copy-start.2
  0.8 0.1 mul.52
  0.9 0.6 copy-done.2
  1.5 0.3 fusion.5
  1.8 0.0 copy-start.1
  1.8 0.7 pad_maximum_fusion.refs_3_
  2.5 0.7 fusion.8.refs_2_
  3.2 0.0 copy-done.1
  3.2 0.1 copy.16
  3.3 0.1 copy.15
  3.4 0.0 copy-start
  3.4 0.7 maximum_maximum_fusion.refs_1_
  4.1 0.1 copy-done
  4.2 0.8 reshape.148
  5.0 0.6 copy.14
  5.6 0.7 reshape.149
  6.3 0.6 add_select_fusion.1
  6.9 0.0 copy-start.3
  7.0 0.7 fusion.refs_4_
  7.7 0.0 copy-done.3
  7.7 0.7 broadcast_in_dim.5.refs_7_
  8.3 97.2 %density.1 = bf16[2,8,32,256]{3,2,1,0:T(8,128)(2,1)} custom-call(bf16[128,8,256]{2,1,0:T(8,128)(2,1)} %bitcast.9, bf16[128,64]{1,0:T(8,128)(2,1)} %maximum_maximum_fusion.refs_1_, bf16[8,256]{1,0:T(8,128)(2,1)} %fusion.8.refs_2_, f32[2,128,128]{2,1,0:T(8,128)} %pad_maximum_fusion.refs_3_, bf16[128,256]{1,0:T(8,128)(2,1)} %fusion.refs_4_, ...), custom_call_target="tpu_custom_call" | custom-call | tf_op jit(solution)/shard_map/density/pallas_call | solution.py:399
  105.5 1.8 %bitcast_convert_fusion = f32[2,256,256]{2,1,0:T(8,128)} fusion(bf16[2,8,32,256]{3,2,1,0:T(8,128)(2,1)} %density.1), kind=kLoop, calls=%fused_computation | loop fusion | flops 131072 | bytes 786432 | tf_op jit(solution)/shard_map/convert_element_type | solution.py:81
  (3 shorter events, 0.0 us)
Async XLA Ops:
  0.8 0.7 copy-start.2
  1.8 1.3 %copy-start.1 = (bf16[2,64,32]{1,2,0:T(8,128)(2,1)S(1)}, bf16[2,64,32]{1,2,0:T(8,128)(2,1)}, u32[]{:S(2)}) copy-start(bf16[2,64,32]{1,2,0:T(8,128)(2,1)} %param.10) | copy-start | bytes 24580
  3.4 0.8 copy-start
  6.9 0.7 copy-start.3

commit v3 on v2

--- a/solution.py
+++ b/solution.py
@@ -65,6 +65,24 @@
     return order.reshape(128, 128)
 
 
+def column_forms():
+    expand = np.zeros((2, NI, 2, 2, 4, 2, 4, 2, NI), np.float32)
+    keep = np.zeros((4, 2, 2, STICK, 4, 2, 4, 2, NI), np.float32)
+    fold = np.zeros((2, STICK, 4, 2, 2, STICK), np.float32)
+    for half in range(2):
+        for i in range(NI):
+            for octet in range(2):
+                for bit in range(2):
+                    expand[half, i, octet, bit, 2 * half + octet, bit, :, :, i] = 1.0
+    for bits in range(4):
+        for y in range(2):
+            keep[bits, :, y, :, :, :, bits, y, :] = 1.0
+    for y in range(2):
+        for s in range(STICK):
+            fold[y, s, :, y, :, s] = 1.0
+    return expand.reshape(64, 512), keep.reshape(128, 512), fold.reshape(16, 128)
+
+
 def dot(a, b):
     return jnp.dot(a, b, preferred_element_type=jnp.float32)
 
@@ -85,21 +103,25 @@
     scale,
     coeffs,
     rotation,
-    live,
-    phase,
-    picked,
-    xs,
-    ys,
-    share_own,
+    lengths,
+    columns,
+    planes,
+    occupation,
     table,
     choice,
     order,
+    expand,
+    only,
+    fold,
     out,
     send,
     recv,
     staged,
     sticks,
     turned,
+    xs,
+    ys,
+    share_own,
     spread,
     hits,
     total,
@@ -142,20 +164,48 @@
     def _(p):
         pl.semaphore_signal(barrier, inc=1, device_id=near((q + p) % NQ), device_id_type=MESH)
 
-    by_stick = narrow(jnp.swapaxes(wide(coeffs[...]), 0, 1))
-    forms = narrow(dot_across(choice[...], rotation[...]))
-    for s in range(STICK):
-        rotated = wide(narrow(dot(forms, by_stick[s])) * live[s : s + 1, :])
-        for t in range(2):
-            turned[:, s, :, t * GRID : (t + 1) * GRID] = rotated[t * 64 : t * 64 + 64].reshape(
-                NI, VALS, GRID
+    for b in range(2):
+        share_own[b] = jnp.zeros((8, 128), jnp.float32) + wide(occupation[b])
+
+    with jax.named_scope("transform"):
+        real, imag = rotation[0], rotation[1]
+        to_real, to_imag = choice[:, 0:32], choice[:, 32:64]
+        forms = jnp.concatenate(
+            [
+                dot(to_real, real) + dot(to_imag, imag),
+                dot(to_imag, real) - dot(to_real, imag),
+            ],
+            1,
+        )
+        forms = narrow(forms)
+        by_stick = narrow(jnp.swapaxes(wide(coeffs[...]), 0, 1))
+        first_row = (lax.axis_index("band") * lax.axis_size("pw") + lax.axis_index("pw")) * STICK
+        at_j = lax.broadcasted_iota(jnp.int32, (1, GRID), 1)
+        lane_stick = lax.broadcasted_iota(jnp.int32, (1, 128), 1) % 64 // VALS
+        shift = jnp.zeros((1, 128), jnp.int32)
+        for s in range(STICK):
+            length = lengths[first_row + s]
+            shift = jnp.where(lane_stick == s, length // 2, shift)
+            live = jnp.where(at_j < length, 1.0, 0.0)
+            rotated = wide(narrow(dot(forms, by_stick[s]))) * live
+            for t in range(2):
+                turned[:, s, :, t * GRID : (t + 1) * GRID] = rotated[
+                    t * 64 : t * 64 + 64
+                ].reshape(NI, VALS, GRID)
+        rows = narrow(turned[...].reshape(NI * STICK * VALS, 2 * GRID))
+        plane = jnp.broadcast_to(wide(planes[...]), (128, 128)).T.astype(jnp.int32)
+        lane = lax.broadcasted_iota(jnp.int32, (128, 128), 1)
+        picked = narrow(
+            jnp.concatenate(
+                [jnp.where(plane == lane, 1.0, 0.0), jnp.where(plane == lane + 128, 1.0, 0.0)], 1
             )
-    rows = narrow(turned[...].reshape(NI * STICK * VALS, 2 * GRID))
-    waves0 = narrow(dot(picked[...], table[0:GRID, :]))
-    waves1 = narrow(dot(picked[...], table[GRID : 2 * GRID, :]))
-    cos = jnp.concatenate([phase[0]] * 4, 1)
-    sin = jnp.concatenate([phase[1]] * 4, 1)
-    values = dot_across(waves0, rows) * cos + dot_across(waves1, rows) * sin
+        )
+        waves0 = narrow(dot(picked, table[0:GRID, :]))
+        waves1 = narrow(dot(picked, table[GRID : 2 * GRID, :]))
+        angle = wide(plane * shift % GRID) * (2.0 * math.pi / GRID)
+        cos = jnp.concatenate([jnp.cos(angle)] * 4, 1)
+        sin = jnp.concatenate([jnp.sin(angle)] * 4, 1)
+        values = dot_across(waves0, rows) * cos + dot_across(waves1, rows) * sin
     values = dot(order[...], narrow(values))
     left = lax.broadcasted_iota(jnp.int32, (16, 128), 1) < 64
     for b in range(4):
@@ -166,7 +216,17 @@
             send[at] = narrow(jnp.where(left, lower, pltpu.roll(upper, 64, 1)))
             send[at + 1] = narrow(jnp.where(left, pltpu.roll(lower, 64, 1), upper))
 
-    pl.semaphore_wait(barrier, NZ + NQ - 2)
+    with jax.named_scope("columns"):
+        natural = wide(columns[...]).T.astype(jnp.int32)
+        for part_of, into in ((natural // GRID, xs), (natural % GRID, ys)):
+            moved = dot(narrow(wide(part_of)), expand[...])
+            moved = dot(fold[...], narrow(moved * wide(only[...]))).astype(jnp.int32)
+            for b in range(4):
+                into[b] = moved[:, b * 128 : b * 128 + 128]
+        total[...] = jnp.zeros_like(total)
+
+    with jax.named_scope("entry"):
+        pl.semaphore_wait(barrier, NZ + NQ - 2)
 
     def first(slot_src, slot_dst, target):
         return pltpu.make_async_remote_copy(
@@ -206,10 +266,12 @@
     keep.start()
     keep.wait()
 
-    @pl.loop(1, NQ)
-    def _(p):
-        t = (q + NQ - p) % NQ
-        first(t, t, near(t)).wait_recv()
+    with jax.named_scope("near"):
+
+        @pl.loop(1, NQ)
+        def _(p):
+            t = (q + NQ - p) % NQ
+            first(t, t, near(t)).wait_recv()
 
     swapped = jnp.swapaxes(wide(recv[...]), 0, 1)
     lower, upper = swapped[:, :16], swapped[:, 16:]
@@ -230,39 +292,35 @@
     def _(step):
         octet = (z // 8 + step + step // 2 - 2 * (step // 3)) % 4
 
-        @pl.loop(0, 8)
-        def _(p):
-            t = octet * 8 + p
-
-            @pl.when(t != z)
-            def _():
-                second(t, t, far(t)).wait_recv()
-
-        block = wide(sticks[pl.ds(octet * 8, 8)].reshape(128, 128)).T
-        held_rows = block.reshape(16, VALS, 128)
-        shares_rows = narrow(held_rows)
-        for b in range(16):
+        with jax.named_scope("arrive"):
+
+            @pl.loop(0, 8)
+            def _(p):
+                t = octet * 8 + p
+
+                @pl.when(t != z)
+                def _():
+                    second(t, t, far(t)).wait_recv()
+
+        with jax.named_scope("scatter"):
+            block = wide(sticks[pl.ds(octet * 8, 8)].reshape(128, 128)).T
+            value = narrow(block.reshape(16, VALS, 128))
             grid_at = lax.broadcasted_iota(jnp.int32, (GRID, 128), 0)
-            hit_x = narrow(jnp.where(grid_at == xs[octet, b : b + 1, :], 1.0, 0.0))
-            hit_y = narrow(jnp.where(grid_at == ys[octet, b : b + 1, :], 1.0, 0.0))
-            hits[:, b * 128 : b * 128 + 128] = hit_x
-            for v in range(VALS):
-                spread[v * GRID : (v + 1) * GRID, b * 128 : b * 128 + 128] = (
-                    hit_y * shares_rows[b, v : v + 1, :]
-                )
-
-        @pl.loop(0, 4)
-        def _(m):
-            at = pl.ds(pl.multiple_of(m * 512, 512), 512)
-            product = dot_across(spread[at, :], hits[...])
-
-            @pl.when(step == 0)
-            def _():
-                total[at, :] = product
-
-            @pl.when(step != 0)
-            def _():
-                total[at, :] += product
+            for b in range(16):
+                at = slice(b * 128, b * 128 + 128)
+                hit = jnp.where(grid_at == xs[octet, b : b + 1, :], 1.0, 0.0)
+                hits[0, :, at] = narrow(hit)
+                hit = jnp.where(grid_at == ys[octet, b : b + 1, :], 1.0, 0.0)
+                hits[1, :, at] = narrow(hit)
+            for m in range(4):
+                for v in (2 * m, 2 * m + 1):
+                    for b in range(16):
+                        at = slice(b * 128, b * 128 + 128)
+                        spread[v * GRID : (v + 1) * GRID, at] = (
+                            hits[1, :, at] * value[b, v : v + 1, :]
+                        )
+                at = slice(m * 512, m * 512 + 512)
+                total[at, :] += dot_across(spread[at, :], hits[0])
 
     weights.wait_recv()
     low = z < 16
@@ -277,11 +335,8 @@
         here, there = share_own[b % 2, 0:1, :], share_other[b % 2, 0:1, :]
         weight = jnp.where(low, here, there) if b < 2 else jnp.where(low, there, here)
         term = power * (jnp.concatenate([weight, weight], 1) * scale)
-        term = term.reshape(NI, HIGH, GRID)
-        if b == 0:
-            part[...] = term
-        else:
-            part[...] += term
+        dens = term if b == 0 else dens + term
+    part[...] = narrow(dens.reshape(NI, HIGH, GRID))
 
     def share(src, dst, t):
         return pltpu.make_async_remote_copy(
@@ -300,14 +355,16 @@
 
     shares[i] = part[i]
 
-    @pl.loop(1, NI)
-    def _(p):
-        t = (i + NI - p) % NI
-        share(t, t, t).wait_recv()
-
-    summed = shares[0]
+    with jax.named_scope("shares"):
+
+        @pl.loop(1, NI)
+        def _(p):
+            t = (i + NI - p) % NI
+            share(t, t, t).wait_recv()
+
+    summed = wide(shares[0])
     for t in range(1, NI):
-        summed = summed + shares[t]
+        summed = summed + wide(shares[t])
     mine[...] = narrow(summed)
     slot = parity(z)
     up, down = (z + 8) % NZ, (z + 24) % NZ
@@ -336,7 +393,8 @@
         )
 
     for k in range(2):
-        hop(0, k, up).wait_recv()
+        with jax.named_scope("hop"):
+            hop(0, k, up).wait_recv()
 
         @pl.loop(1, NI)
         def _(p):
@@ -345,12 +403,13 @@
 
         out[k, i] = held[k]
 
-    for k in range(2):
-
-        @pl.loop(1, NI)
-        def _(p):
-            t = (i + NI - p) % NI
-            spread_out(k, t, t).wait_recv()
+    with jax.named_scope("gather"):
+        for k in range(2):
+
+            @pl.loop(1, NI)
+            def _(p):
+                t = (i + NI - p) % NI
+                spread_out(k, t, t).wait_recv()
 
     weights.wait_send()
     hop(0, slot, up).wait_send()
@@ -376,30 +435,15 @@
 
 def shards(coeffs, rotation_matrix, stick_length, stick_column, plane_index, occupation):
     band_count = lax.axis_size("band")
-    row = lax.axis_index("band") * lax.axis_size("pw") + lax.axis_index("pw")
-    lengths = lax.dynamic_slice_in_dim(stick_length, row * STICK, STICK)
-    real, imag = rotation_matrix[0], rotation_matrix[1]
-    rotation = jnp.concatenate(
-        [jnp.concatenate([real, imag], 1), jnp.concatenate([-imag, real], 1)], 0
-    )
-    at = jnp.arange(GRID, dtype=jnp.int32)
-    live = narrow(at[None, :] < lengths[:, None])
-    shift = jnp.broadcast_to((lengths // 2)[None, :, None], (2, STICK, VALS)).reshape(1, 128)
-    product = plane_index[:, None] * shift % GRID
-    angle = 2.0 * math.pi / GRID * wide(product)
-    phase = jnp.stack([jnp.cos(angle), jnp.sin(angle)])
-    picked = narrow(plane_index[:, None] == at[None, :])
-    column = stick_column.reshape(2, NI, 2, 8, 2, 2, STICK)
-    column = jnp.transpose(column, (0, 2, 4, 6, 3, 5, 1)).reshape(4, 16, 128)
-    weights = jnp.broadcast_to(wide(occupation)[:, None, None], (2, 8, 128))
     scale = 1.0 / float(occupation.shape[0] * band_count * stick_column.shape[0] * GRID)
     vmem = pl.BlockSpec(memory_space=pltpu.VMEM)
+    smem = pl.BlockSpec(memory_space=pltpu.SMEM)
     dma = pltpu.SemaphoreType.DMA
     bf16, f32 = jnp.bfloat16, jnp.float32
     result = pl.pallas_call(
         lambda *refs: kernel(scale, *refs),
         out_shape=jax.ShapeDtypeStruct((2, NI, HIGH, GRID), bf16),
-        in_specs=[vmem] * 11,
+        in_specs=[vmem, vmem, smem, vmem, vmem, smem] + [vmem] * 6,
         out_specs=vmem,
         scratch_shapes=[
             pltpu.VMEM((NQ, 16, 128), bf16),
@@ -407,12 +451,15 @@
             pltpu.VMEM((NZ, 16, 128), bf16),
             pltpu.VMEM((NZ, 16, 128), bf16),
             pltpu.VMEM((NI, STICK, VALS, 2 * GRID), f32),
+            pltpu.VMEM((4, 16, 128), jnp.int32),
+            pltpu.VMEM((4, 16, 128), jnp.int32),
+            pltpu.VMEM((2, 8, 128), f32),
             pltpu.VMEM((VALS * GRID, OCTET), bf16),
-            pltpu.VMEM((GRID, OCTET), bf16),
+            pltpu.VMEM((2, GRID, OCTET), bf16),
             pltpu.VMEM((VALS * GRID, GRID), f32),
             pltpu.VMEM((GRID, 2 * GRID), bf16),
-            pltpu.VMEM((NI, HIGH, GRID), f32),
-            pltpu.VMEM((NI, HIGH, GRID), f32),
+            pltpu.VMEM((NI, HIGH, GRID), bf16),
+            pltpu.VMEM((NI, HIGH, GRID), bf16),
             pltpu.VMEM((HIGH, GRID), bf16),
             pltpu.VMEM((2, HIGH, GRID), bf16),
             pltpu.VMEM((2, 8, 128), f32),
@@ -436,16 +483,13 @@
         name="density",
     )(
         coeffs.reshape(128, STICK, GRID),
-        rotation,
-        live,
-        phase,
-        picked,
-        column // GRID,
-        column % GRID,
-        weights,
-        jnp.asarray(fourier(), bf16),
-        jnp.asarray(band_choice(), bf16),
-        jnp.asarray(plane_order(), bf16),
+        jnp.transpose(rotation_matrix, (0, 2, 1)),
+        stick_length,
+        stick_column.reshape(64, 128),
+        plane_index.reshape(1, 128),
+        occupation,
+        *(jnp.asarray(form, bf16) for form in (fourier(), band_choice(), plane_order())),
+        *(jnp.asarray(form, bf16) for form in column_forms()),
     )
     return wide(result.reshape(2, GRID, GRID))
 

time: 108 us -> 86.5 us (0.80)
  Pallas kernels: 97.2 us -> 84.6 us
  other arithmetic: 6.25 us -> 1.78 us
  local copies, waits for them, and re-layouts: 3.8 us -> 0 us
    pallas_call x1, Pallas kernels: 97.2 us -> 84.6 us  [shards(): pl.pallas_call(lambda *refs: kernel(scale, *refs), out_shape=jax.ShapeDty...]
    reshape x2 -> x0, local copies, waits for them, and re-layouts: 1.5 us -> none  [the longest x1 0.8 us: shards(): column = stick_column.reshape(2, NI, 2, 8, 2, 2, STICK)]
    select_n x2 -> x0, other arithmetic: 1.41 us -> none  [the longest x1 0.77 us: shards(): lengths // 2]
    convert_element_type x2 -> x0, other arithmetic: 1.36 us -> none  [narrow(): return a.astype(jnp.bfloat16)]
where the time goes in v3:
time: 86.5 us; the launch traced here: 86.4 us
  Pallas kernels  84.6 us (98%)
  other arithmetic  1.78 us (2%)
    pallas_call x1, Pallas kernels, shards(): pl.pallas_call(lambda *refs: kernel(scale, *refs), out_shape=jax.ShapeDty...  84.6 us
    convert_element_type x1, other arithmetic, wide(): return a.astype(jnp.float32)  1.78 us

profile of v3, /device:TPU:1, one launch (start us, length us, event | category | flops | bytes accessed | tf_op | source)
XLA Modules:
  0.0 86.4 jit_solution(971390116133381175)
XLA Ops:
  0.0 84.6 %density.1 = bf16[2,8,32,256]{3,2,1,0:T(8,128)(2,1)} custom-call(bf16[128,8,256]{2,1,0:T(8,128)(2,1)} %bitcast.7, bf16[2,32,64]{2,1,0:T(8,128)(2,1)} %bitcast.9, s32[8192]{0:T(1024)} %refs_2_.1, s32[64,128]{1,0:T(8,128)} %bitcast.8, s32[1,128]{1,0:T(1,128)} %bitcast.10, s32[2]{0:T(128)} %refs_5_.1, bf16[512,512]{1,0:T(8,128)(2,1)} %constant.12.clone.refs_6_, ...), custom_call_target="tpu_custom_call" | custom-call | tf_op jit(solution)/shard_map/density/pallas_call | solution.py:443
  84.6 1.8 %bitcast_convert_fusion = f32[2,256,256]{2,1,0:T(8,128)} fusion(bf16[2,8,32,256]{3,2,1,0:T(8,128)(2,1)} %density.1), kind=kLoop, calls=%fused_computation | loop fusion | flops 131072 | bytes 786432 | tf_op jit(solution)/shard_map/convert_element_type | solution.py:99

commit v4 on v3

--- a/solution.py
+++ b/solution.py
@@ -101,50 +101,11 @@
 
 def kernel(
     scale,
-    coeffs,
-    rotation,
-    lengths,
-    columns,
-    planes,
-    occupation,
-    table,
-    choice,
-    order,
-    expand,
-    only,
-    fold,
-    out,
-    send,
-    recv,
-    staged,
-    sticks,
-    turned,
-    xs,
-    ys,
-    share_own,
-    spread,
-    hits,
-    total,
-    half,
-    part,
-    shares,
-    mine,
-    held,
-    share_other,
-    s1,
-    r1,
-    s2,
-    r2,
-    s3,
-    r3,
-    s4,
-    r4,
-    s5,
-    r5,
-    own,
-    s6,
-    r6,
+    *refs,
 ):
+    given, out, fetched, rest = refs[:12], refs[12], refs[13:25], refs[25:]
+    (coeffs, rotation, lengths, columns, planes, occupation, table, choice, order, expand, only, fold) = fetched
+    (send, recv, staged, sticks, turned, xs, ys, share_own, spread, hit_x, hit_y, total, half, part, shares, mine, held, share_other, s1, r1, s2, r2, s3, r3, s4, r4, s5, r5, own, s6, r6, fetch, word) = rest
     z, y, i = place()
     q = y * NI + i
 
@@ -156,14 +117,30 @@
 
     barrier = pltpu.get_barrier_semaphore()
 
-    @pl.loop(1, NZ)
-    def _(p):
-        pl.semaphore_signal(barrier, inc=1, device_id=far((z + p) % NZ), device_id_type=MESH)
-
     @pl.loop(1, NQ)
     def _(p):
         pl.semaphore_signal(barrier, inc=1, device_id=near((q + p) % NQ), device_id_type=MESH)
 
+    @pl.loop(1, 5)
+    def _(p):
+        for t in ((z + p) % NZ, (z + NZ - p) % NZ):
+            pl.semaphore_signal(barrier, inc=1, device_id=far(t), device_id_type=MESH)
+
+    def tell(n, distance):
+        for t in ((z + distance) % NZ, (z + NZ - distance) % NZ):
+            pl.semaphore_signal(word.at[n], inc=1, device_id=far(t), device_id_type=MESH)
+
+    def hear(n):
+        pl.semaphore_wait(word.at[n], 2)
+
+    fetches = [
+        pltpu.make_async_copy(source, target, fetch.at[n])
+        for n, (source, target) in enumerate(zip(given, fetched))
+    ]
+    for copy in fetches:
+        copy.start()
+    for copy in fetches:
+        copy.wait()
     for b in range(2):
         share_own[b] = jnp.zeros((8, 128), jnp.float32) + wide(occupation[b])
 
@@ -193,6 +170,8 @@
                     t * 64 : t * 64 + 64
                 ].reshape(NI, VALS, GRID)
         rows = narrow(turned[...].reshape(NI * STICK * VALS, 2 * GRID))
+        pl.semaphore_wait(barrier, NQ + 7)
+        tell(0, 4)
         plane = jnp.broadcast_to(wide(planes[...]), (128, 128)).T.astype(jnp.int32)
         lane = lax.broadcasted_iota(jnp.int32, (128, 128), 1)
         picked = narrow(
@@ -216,18 +195,6 @@
             send[at] = narrow(jnp.where(left, lower, pltpu.roll(upper, 64, 1)))
             send[at + 1] = narrow(jnp.where(left, pltpu.roll(lower, 64, 1), upper))
 
-    with jax.named_scope("columns"):
-        natural = wide(columns[...]).T.astype(jnp.int32)
-        for part_of, into in ((natural // GRID, xs), (natural % GRID, ys)):
-            moved = dot(narrow(wide(part_of)), expand[...])
-            moved = dot(fold[...], narrow(moved * wide(only[...]))).astype(jnp.int32)
-            for b in range(4):
-                into[b] = moved[:, b * 128 : b * 128 + 128]
-        total[...] = jnp.zeros_like(total)
-
-    with jax.named_scope("entry"):
-        pl.semaphore_wait(barrier, NZ + NQ - 2)
-
     def first(slot_src, slot_dst, target):
         return pltpu.make_async_remote_copy(
             src_ref=send.at[slot_src],
@@ -253,6 +220,21 @@
         t = (q + p) % NQ
         first(t, q, near(t)).start()
 
+    hear(0)
+    tell(1, 8)
+    with jax.named_scope("columns"):
+        natural = wide(columns[...]).T.astype(jnp.int32)
+        into = []
+        for part_of in (natural // GRID, natural % GRID):
+            moved = dot(narrow(wide(part_of)), expand[...])
+            moved = dot(fold[...], narrow(moved * wide(only[...])))
+            into.append(moved)
+        for n in range(4):
+            part_of = jnp.concatenate([into[0][:, n * 128 : n * 128 + 128]] * 8, 0).T
+            xs[n] = part_of.astype(jnp.int32)
+            ys[n] = into[1][:, n * 128 : n * 128 + 128].astype(jnp.int32)
+        total[...] = jnp.zeros_like(total)
+
     weights = pltpu.make_async_remote_copy(
         src_ref=share_own,
         dst_ref=share_other,
@@ -261,7 +243,6 @@
         device_id=far((z + 16) % NZ),
         device_id_type=MESH,
     )
-    weights.start()
     keep = pltpu.make_async_copy(send.at[q], recv.at[q], own.at[0])
     keep.start()
     keep.wait()
@@ -279,7 +260,16 @@
     staged[0:16] = narrow(jnp.where(left, lower, pltpu.roll(upper, 64, 2)))
     staged[16:32] = narrow(jnp.where(left, pltpu.roll(lower, 64, 2), upper))
 
-    @pl.loop(1, NZ)
+    hear(1)
+    weights.start()
+
+    @pl.loop(1, 7)
+    def _(p):
+        away = (p + 1) // 2
+        t = (z + p % 2 * away + (1 - p % 2) * (NZ - away)) % NZ
+        second(t, z, far(t)).start()
+
+    @pl.loop(1, NZ - 6)
     def _(p):
         t = (z + (16 + p // 2 * (1 - p % 2 * 2))) % NZ
         second(t, z, far(t)).start()
@@ -288,9 +278,22 @@
     keep2.start()
     keep2.wait()
 
+    with jax.named_scope("where"):
+
+        @pl.loop(0, 4)
+        def _(n):
+            down = lax.broadcasted_iota(jnp.int32, (GRID, 128), 0)
+            right = lax.broadcasted_iota(jnp.int32, (128, GRID), 1)
+            for b in range(16):
+                at = slice(b * 128, b * 128 + 128)
+                hit = jnp.where(right == xs[n, :, b : b + 1], 1.0, 0.0)
+                hit_x[n, at, :] = narrow(hit)
+                hit = jnp.where(down == ys[n, b : b + 1, :], 1.0, 0.0)
+                hit_y[n, :, at] = narrow(hit)
+
     @pl.loop(0, 4)
     def _(step):
-        octet = (z // 8 + step + step // 2 - 2 * (step // 3)) % 4
+        octet = (z // 8 + step * 2 % 3 + step // 3 * 3) % 4
 
         with jax.named_scope("arrive"):
 
@@ -305,22 +308,15 @@
         with jax.named_scope("scatter"):
             block = wide(sticks[pl.ds(octet * 8, 8)].reshape(128, 128)).T
             value = narrow(block.reshape(16, VALS, 128))
-            grid_at = lax.broadcasted_iota(jnp.int32, (GRID, 128), 0)
-            for b in range(16):
-                at = slice(b * 128, b * 128 + 128)
-                hit = jnp.where(grid_at == xs[octet, b : b + 1, :], 1.0, 0.0)
-                hits[0, :, at] = narrow(hit)
-                hit = jnp.where(grid_at == ys[octet, b : b + 1, :], 1.0, 0.0)
-                hits[1, :, at] = narrow(hit)
             for m in range(4):
                 for v in (2 * m, 2 * m + 1):
                     for b in range(16):
                         at = slice(b * 128, b * 128 + 128)
                         spread[v * GRID : (v + 1) * GRID, at] = (
-                            hits[1, :, at] * value[b, v : v + 1, :]
+                            hit_y[octet, :, at] * value[b, v : v + 1, :]
                         )
                 at = slice(m * 512, m * 512 + 512)
-                total[at, :] += dot_across(spread[at, :], hits[0])
+                total[at, :] += dot(spread[at, :], hit_x[octet])
 
     weights.wait_recv()
     low = z < 16
@@ -436,26 +432,40 @@
 def shards(coeffs, rotation_matrix, stick_length, stick_column, plane_index, occupation):
     band_count = lax.axis_size("band")
     scale = 1.0 / float(occupation.shape[0] * band_count * stick_column.shape[0] * GRID)
+    bf16, f32 = jnp.bfloat16, jnp.float32
     vmem = pl.BlockSpec(memory_space=pltpu.VMEM)
-    smem = pl.BlockSpec(memory_space=pltpu.SMEM)
+    given = (
+        coeffs.reshape(128, STICK, GRID),
+        jnp.transpose(rotation_matrix, (0, 2, 1)),
+        stick_length,
+        stick_column.reshape(64, 128),
+        plane_index.reshape(1, 128),
+        occupation,
+        *(jnp.asarray(form, bf16) for form in (fourier(), band_choice(), plane_order())),
+        *(jnp.asarray(form, bf16) for form in column_forms()),
+    )
     dma = pltpu.SemaphoreType.DMA
-    bf16, f32 = jnp.bfloat16, jnp.float32
     result = pl.pallas_call(
         lambda *refs: kernel(scale, *refs),
         out_shape=jax.ShapeDtypeStruct((2, NI, HIGH, GRID), bf16),
-        in_specs=[vmem, vmem, smem, vmem, vmem, smem] + [vmem] * 6,
+        in_specs=[pl.BlockSpec(memory_space=pl.ANY)] * len(given),
         out_specs=vmem,
         scratch_shapes=[
+            *(
+                (pltpu.SMEM if n in (2, 5) else pltpu.VMEM)(form.shape, form.dtype)
+                for n, form in enumerate(given)
+            ),
             pltpu.VMEM((NQ, 16, 128), bf16),
             pltpu.VMEM((NQ, 16, 128), bf16),
             pltpu.VMEM((NZ, 16, 128), bf16),
             pltpu.VMEM((NZ, 16, 128), bf16),
             pltpu.VMEM((NI, STICK, VALS, 2 * GRID), f32),
-            pltpu.VMEM((4, 16, 128), jnp.int32),
+            pltpu.VMEM((4, 128, 128), jnp.int32),
             pltpu.VMEM((4, 16, 128), jnp.int32),
             pltpu.VMEM((2, 8, 128), f32),
             pltpu.VMEM((VALS * GRID, OCTET), bf16),
-            pltpu.VMEM((2, GRID, OCTET), bf16),
+            pltpu.VMEM((4, OCTET, GRID), bf16),
+            pltpu.VMEM((4, GRID, OCTET), bf16),
             pltpu.VMEM((VALS * GRID, GRID), f32),
             pltpu.VMEM((GRID, 2 * GRID), bf16),
             pltpu.VMEM((NI, HIGH, GRID), bf16),
@@ -476,21 +486,14 @@
             dma((2,)),
             dma,
             dma,
+            dma((len(given),)),
+            pltpu.SemaphoreType.REGULAR((2,)),
         ],
         compiler_params=pltpu.CompilerParams(
             collective_id=1, has_side_effects=True, vmem_limit_bytes=VMEM_LIMIT
         ),
         name="density",
-    )(
-        coeffs.reshape(128, STICK, GRID),
-        jnp.transpose(rotation_matrix, (0, 2, 1)),
-        stick_length,
-        stick_column.reshape(64, 128),
-        plane_index.reshape(1, 128),
-        occupation,
-        *(jnp.asarray(form, bf16) for form in (fourier(), band_choice(), plane_order())),
-        *(jnp.asarray(form, bf16) for form in column_forms()),
-    )
+    )(*given)
     return wide(result.reshape(2, GRID, GRID))
 
 

time: 86.5 us -> 82.7 us (0.956)
  Pallas kernels: 84.6 us -> 80.7 us
    pallas_call x1, Pallas kernels: 84.6 us -> 80.7 us  [shards(): pl.pallas_call(lambda *refs: kernel(scale, *refs), out_shape=jax.ShapeDty...]
where the time goes in v4:
time: 82.7 us; the launch traced here: 82.5 us
  Pallas kernels  80.7 us (98%)
  other arithmetic  1.78 us (2%)
    pallas_call x1, Pallas kernels, shards(): pl.pallas_call(lambda *refs: kernel(scale, *refs), out_shape=jax.ShapeDty...  80.7 us
    convert_element_type x1, other arithmetic, wide(): return a.astype(jnp.float32)  1.78 us

profile of v4, /device:TPU:1, one launch (start us, length us, event | category | flops | bytes accessed | tf_op | source)
XLA Modules:
  0.0 82.5 jit_solution(75818662986885879)
XLA Ops:
  0.0 80.7 %density.1 = bf16[2,8,32,256]{3,2,1,0:T(8,128)(2,1)} custom-call(bf16[128,8,256]{2,1,0:T(8,128)(2,1)} %bitcast.7, bf16[2,32,64]{2,1,0:T(8,128)(2,1)} %bitcast.9, s32[8192]{0:T(1024)} %refs_2_.1, s32[64,128]{1,0:T(8,128)} %bitcast.8, s32[1,128]{1,0:T(1,128)} %bitcast.10, s32[2]{0:T(128)} %refs_5_.1, bf16[512,512]{1,0:T(8,128)(2,1)} %constant.12.clone.refs_6_, ...), custom_call_target="tpu_custom_call" | custom-call | tf_op jit(solution)/shard_map/density/pallas_call | solution.py:448
  80.7 1.8 %bitcast_convert_fusion = f32[2,256,256]{2,1,0:T(8,128)} fusion(bf16[2,8,32,256]{3,2,1,0:T(8,128)(2,1)} %density.1), kind=kLoop, calls=%fused_computation | loop fusion | flops 131072 | bytes 786432 | tf_op jit(solution)/shard_map/convert_element_type | solution.py:99

commit v5 on v4

--- a/solution.py
+++ b/solution.py
@@ -263,15 +263,10 @@
     hear(1)
     weights.start()
 
-    @pl.loop(1, 7)
+    @pl.loop(1, NZ)
     def _(p):
         away = (p + 1) // 2
         t = (z + p % 2 * away + (1 - p % 2) * (NZ - away)) % NZ
-        second(t, z, far(t)).start()
-
-    @pl.loop(1, NZ - 6)
-    def _(p):
-        t = (z + (16 + p // 2 * (1 - p % 2 * 2))) % NZ
         second(t, z, far(t)).start()
 
     keep2 = pltpu.make_async_copy(staged.at[z], sticks.at[z], own.at[1])
@@ -293,7 +288,7 @@
 
     @pl.loop(0, 4)
     def _(step):
-        octet = (z // 8 + step * 2 % 3 + step // 3 * 3) % 4
+        octet = (z // 8 + step + step // 2 - 2 * (step // 3)) % 4
 
         with jax.named_scope("arrive"):
 

time: 82.7 us -> 86 us (1.040)
  Pallas kernels: 80.7 us -> 84 us
    pallas_call x1, Pallas kernels: 80.7 us -> 84 us  [shards(): pl.pallas_call(lambda *refs: kernel(scale, *refs), out_shape=jax.ShapeDty...]
where the time goes in v5:
time: 86 us; the launch traced here: 85.8 us
  Pallas kernels  84 us (98%)
  other arithmetic  1.78 us (2%)
    pallas_call x1, Pallas kernels, shards(): pl.pallas_call(lambda *refs: kernel(scale, *refs), out_shape=jax.ShapeDty...  84 us
    convert_element_type x1, other arithmetic, wide(): return a.astype(jnp.float32)  1.78 us

profile of v5, /device:TPU:1, one launch (start us, length us, event | category | flops | bytes accessed | tf_op | source)
XLA Modules:
  0.0 85.8 jit_solution(7535959737093621732)
XLA Ops:
  0.0 84.0 %density.1 = bf16[2,8,32,256]{3,2,1,0:T(8,128)(2,1)} custom-call(bf16[128,8,256]{2,1,0:T(8,128)(2,1)} %bitcast.7, bf16[2,32,64]{2,1,0:T(8,128)(2,1)} %bitcast.9, s32[8192]{0:T(1024)} %refs_2_.1, s32[64,128]{1,0:T(8,128)} %bitcast.8, s32[1,128]{1,0:T(1,128)} %bitcast.10, s32[2]{0:T(128)} %refs_5_.1, bf16[512,512]{1,0:T(8,128)(2,1)} %constant.12.clone.refs_6_, ...), custom_call_target="tpu_custom_call" | custom-call | tf_op jit(solution)/shard_map/density/pallas_call | solution.py:443
  84.0 1.8 %bitcast_convert_fusion = f32[2,256,256]{2,1,0:T(8,128)} fusion(bf16[2,8,32,256]{3,2,1,0:T(8,128)(2,1)} %density.1), kind=kLoop, calls=%fused_computation | loop fusion | flops 131072 | bytes 786432 | tf_op jit(solution)/shard_map/convert_element_type | solution.py:99
